TPU v7x, 512 devices: a whole 4x4x16 slice. The times are simulated.
512 devices in a mesh: pool: 64 (over z, y), head: 8 (over x, core).
Axes of the slice: x: 4, y: 4, z: 16, core: 2. Of those that a mesh axis runs over, the one named last changes fastest.
Arguments:
- kv_store: bfloat16 [128, 2, 64, 1024], P('pool', None, None, 'head'), may hold values from -6 to 6
- fresh_q: bfloat16 [64, 24, 8192], P('pool', None, 'head'), may hold values from -160 to 160
- fresh_kv: bfloat16 [64, 24, 2, 1024], P('pool', None, None, 'head'), may hold values from -6 to 6
- dec_q: bfloat16 [32, 8192], P(None, 'head'), may hold values from -160 to 160
- dec_kv: bfloat16 [32, 2, 1024], P(None, None, 'head'), may hold values from -6 to 6
- out_weight: bfloat16 [8192, 8192], P('head', 'pool'), may hold values from -0.0625 to 0.0625
- span_slot: int32 [64], replicated, may hold values from 0 to 127, as said below
- span_order: int32 [64], replicated, may hold values from 0 to 63, each once
- span_start: int32 [64], replicated, may hold values from 0 to 4536, as said below
- pick: int32 [64, 24], replicated, may hold values from 0 to 63, as said below
- dec_len: int32 [32], replicated, may hold values from 1 to 64, as said below
Outputs:
- fresh_out: bfloat16 [64, 24, 8192], P('pool', None, 'head')
- dec_proj: bfloat16 [32, 8192], P(None, 'pool')
Inputs may be any that keep to these rules, and one draw needn't show every extreme that they name: `span_slot`: distinct values. Storage rows k * 2 to (k + 1) * 2 - 1 belong to pool device k; some device holds 2 spans in every draw. span_start[0] = 0 and span_start[s + 1] - span_start[s] lies between 64 and 80. `pick`: each row holds 24 distinct indices in increasing order. `dec_len`: some row reads all 64 slots in every draw.
All inputs are finite; a program needn't handle non-finite values.
Results may differ from a plain program's by a relative error of at most 0.018.
Values may be sent and summed in bfloat16 or wider, within the bound.
A program may use at most 64 MiB of HBM per device.

v0:
```python
import jax
import jax.numpy as jnp
from jax import lax
from jax.sharding import PartitionSpec as P

QH = 64
KVH = 8
HD = 128
L = 64
R = 24
NEG = -1e30
BASE = 500000.0


def merged_2(value, axis, combine):
    everything = jax.tree.map(
        lambda part, kind: lax.all_gather(part.astype(kind), axis),
        value,
        jax.tree.map(lambda a: jnp.bfloat16 if a.dtype == jnp.float32 else a.dtype, value),
    )

    def take(k):
        return jax.tree.map(lambda part, own: part[k].astype(own.dtype), everything, value)

    return lax.fori_loop(
        1, lax.axis_size(axis), lambda k, so_far: combine(so_far, take(k)), take(0)
    )


def frequencies(half):
    return jnp.power(BASE, -jnp.arange(half, dtype=jnp.float32) / half)


def rotate(heads, positions):
    half = heads.shape[-1] // 2
    angle = positions.astype(jnp.float32)[:, None, None] * frequencies(half)
    cosine = jnp.cos(angle)
    sine = jnp.sin(angle)
    first = heads[..., :half]
    second = heads[..., half:]
    return jnp.concatenate(
        [first * cosine - second * sine, second * cosine + first * sine], axis=-1
    )


def to_groups(rows_in, group):
    count = rows_in.shape[0]
    shaped = rows_in.reshape(count, -1, group, HD)
    local = shaped.shape[1]
    return shaped.transpose(1, 0, 2, 3).reshape(local, count * group, HD)


def from_groups(merged, count, group):
    local = merged.shape[0]
    return (
        merged.reshape(local, count, group, HD)
        .transpose(1, 0, 2, 3)
        .reshape(count, local * group * HD)
    )


def by_head(rows_in):
    count = rows_in.shape[0]
    return rows_in.reshape(count, -1, HD).transpose(1, 0, 2)


def empty_state(local, count):
    return (
        jnp.full((local, count), NEG, jnp.float32),
        jnp.zeros((local, count), jnp.float32),
        jnp.zeros((local, count, HD), jnp.float32),
    )


def absorb(state, queries, key_block, value_block, visible):
    highest, total, accum = state
    scale = HD ** (-0.5)
    scores = (
        jnp.einsum("gqd,gkd->gqk", queries, key_block, preferred_element_type=jnp.float32) * scale
    )
    scores = jnp.where(visible[None], scores, NEG)
    raised = jnp.maximum(highest, jnp.max(scores, axis=-1))
    weights = jnp.where(visible[None], jnp.exp(scores - raised[..., None]), 0.0)
    factor = jnp.exp(highest - raised)
    total = total * factor + jnp.sum(weights, axis=-1)
    accum = accum * factor[..., None] + jnp.einsum(
        "gqk,gkd->gqd",
        weights.astype(jnp.bfloat16),
        value_block,
        preferred_element_type=jnp.float32,
    )
    return (raised, total, accum)


def combine(first, second):
    raised = jnp.maximum(first[0], second[0])
    left = jnp.exp(first[0] - raised)
    right = jnp.exp(second[0] - raised)
    return (
        raised,
        first[1] * left + second[1] * right,
        first[2] * left[..., None] + second[2] * right[..., None],
    )


def shards(
    kv_store,
    fresh_q,
    fresh_kv,
    dec_q,
    dec_kv,
    out_weight,
    span_slot,
    span_order,
    span_start,
    pick,
    dec_len,
):
    group = QH // KVH
    my_slot = lax.axis_index("pool")
    slots = span_order.shape[0]
    stored = kv_store.shape[0]
    store_total = stored * lax.axis_size("pool")
    local = fresh_kv.shape[-1] // HD
    rows = dec_q.shape[0]
    span_ids = jnp.arange(slots, dtype=jnp.int32)
    span_place = jnp.sum(
        jnp.where(span_order[None, :] == span_ids[:, None], span_ids[None, :], 0), axis=1
    )
    store_ids = jnp.arange(store_total, dtype=jnp.int32)
    holding = span_slot[None, :] == store_ids[:, None]
    store_live = jnp.any(holding, axis=1)
    store_place = jnp.sum(jnp.where(holding, span_place[None, :], 0), axis=1)
    columns = jnp.arange(L, dtype=jnp.int32)
    picked = jnp.any(pick[:, :, None] == columns[None, None, :], axis=1)
    own_pick = lax.dynamic_index_in_dim(pick, my_slot, 0, keepdims=False)
    own_start = lax.dynamic_index_in_dim(span_start, my_slot, 0, keepdims=False)
    query_place = own_start + own_pick
    rotated_q = rotate(fresh_q[0].reshape(R, -1, HD).astype(jnp.float32), query_place).astype(
        jnp.bfloat16
    )
    queries = to_groups(rotated_q.reshape(R, -1), group)
    query_reach = jnp.repeat(query_place, group)
    every_fresh = lax.all_gather(fresh_kv, "pool", axis=0, tiled=True)
    fresh_place = (span_start[:, None] + pick).reshape(-1)
    turned_fresh = rotate(
        every_fresh[:, :, 0].reshape(slots * R, -1, HD).astype(jnp.float32), fresh_place
    ).astype(jnp.bfloat16)
    fresh_keys = by_head(turned_fresh.reshape(slots * R, -1))
    fresh_values = by_head(every_fresh[:, :, 1].reshape(slots * R, -1))
    recompute_state = absorb(
        empty_state(local, R * group),
        queries,
        fresh_keys,
        fresh_values,
        fresh_place[None, :] <= query_reach[:, None],
    )
    dec_queries = to_groups(dec_q, group)
    row_len = jnp.repeat(dec_len, group)

    def view(item, place):
        turned = rotate(
            item[0].reshape(L, -1, HD).astype(jnp.float32), jnp.full((L,), span_start[place])
        ).astype(jnp.bfloat16)
        reach = span_start[place] + columns
        keep = jnp.logical_not(lax.dynamic_index_in_dim(picked, place, 0, keepdims=False))
        return (by_head(turned.reshape(L, -1)), by_head(item[1]), reach, keep)

    initial = (recompute_state,)

    def wanted(place):
        return place <= my_slot

    def block_step(carry, key_block, value_block, reach, keep):
        seen = keep[None, :] & (reach[None, :] <= query_reach[:, None])
        return (absorb(carry[0], queries, key_block, value_block, seen),)

    piece = lax.all_gather(kv_store, "pool", axis=0, tiled=True)

    def one_row(inner, inputs):
        item, index = inputs
        place = store_place[index]

        def apply(state_in):
            key_block, value_block, reach, keep = view(item, place)
            return block_step(state_in, key_block, value_block, reach, keep)

        return (
            lax.cond(store_live[index] & wanted(place), apply, lambda state_in: state_in, inner),
            None,
        )

    indices = jnp.arange(piece.shape[0], dtype=jnp.int32)
    result, _ = lax.scan(one_row, initial, (piece, indices))
    own_keys = lax.dynamic_slice_in_dim(fresh_keys, my_slot * R, R, 1)
    own_values = lax.dynamic_slice_in_dim(fresh_values, my_slot * R, R, 1)
    seen_fresh = jnp.broadcast_to((my_slot < row_len)[:, None], (rows * group, R))
    dec_state = absorb(
        empty_state(local, rows * group), dec_queries, own_keys, own_values, seen_fresh
    )

    def make_apply(item, place):

        def apply(state_in):
            key_block, value_block, reach, keep = view(item, place)
            return absorb(
                state_in,
                dec_queries,
                key_block,
                value_block,
                keep[None, :] & (place < row_len)[:, None],
            )

        return apply

    for offset in range(stored):
        index = my_slot * stored + offset
        place = store_place[index]
        dec_state = lax.cond(
            store_live[index],
            make_apply(kv_store[offset], place),
            lambda state_in: state_in,
            dec_state,
        )
    dec_state = merged_2(dec_state, "pool", combine)
    recompute_final = result[0]
    attended = recompute_final[2] / recompute_final[1][..., None]
    fresh_out = from_groups(attended, R, group).astype(jnp.bfloat16)[None]
    token_keys = by_head(dec_kv[:, 0])
    token_values = by_head(dec_kv[:, 1])
    token_seen = (jnp.arange(rows * group, dtype=jnp.int32) // group)[:, None] == jnp.arange(
        rows, dtype=jnp.int32
    )[None, :]
    dec_state = absorb(dec_state, dec_queries, token_keys, token_values, token_seen)
    dec_attn = from_groups(dec_state[2] / dec_state[1][..., None], rows, group).astype(jnp.bfloat16)
    partial_terms = jnp.dot(dec_attn, out_weight, preferred_element_type=jnp.float32)
    dec_proj = lax.psum(partial_terms, "head").astype(jnp.bfloat16)
    return (fresh_out, dec_proj)


def solution(mesh):
    return jax.shard_map(
        shards,
        mesh=mesh,
        in_specs=(
            P("pool", None, None, "head"),
            P("pool", None, "head"),
            P("pool", None, None, "head"),
            P(None, "head"),
            P(None, None, "head"),
            P("head", "pool"),
            P(),
            P(),
            P(),
            P(),
            P(),
        ),
        out_specs=(P("pool", None, "head"), P(None, "pool")),
        check_vma=False,
    )
```

profile of v0, /device:TPU:504, one launch (start us, length us, event | category | flops | bytes accessed | tf_op | source)
XLA Modules:
  0.0 1444.8 jit_solution(17761273239110863424)
XLA Ops:
  17.9 92.9 %all_gather.24 = bf16[64,24,2,128]{3,1,0,2:T(8,128)(2,1)S(1)} all-gather(bf16[1,24,2,128]{3,1,0,2:T(8,128)(2,1)S(1)} %copy.26), channel_id=1, replica_groups=mesh['pool'=64,'head'=8] {'pool'}, dimensions={0}, use_global_device_ids=true | all-gather | bytes 798720 | tf_op jit(solution)/shard_map/all_gather | solution.py:144
  123.2 84.3 %all-gather.3 = bf16[64,1,256]{2,1,0:T(2,128)(2,1)S(1)} all-gather(bf16[1,1,256]{2,1,0:T(2,128)(2,1)S(1)} %convert_bitcast_fusion.2), channel_id=2, replica_groups=mesh['pool'=64,'head'=8] {'pool'}, dimensions={0}, use_global_device_ids=true | all-gather | bytes 33280 | tf_op jit(solution)/shard_map/all_gather | solution.py:17
  207.5 79.9 %all-gather.4 = bf16[64,1,256]{2,1,0:T(2,128)(2,1)S(1)} all-gather(bf16[1,1,256]{2,1,0:T(2,128)(2,1)S(1)} %convert_bitcast_fusion.1), channel_id=3, replica_groups=mesh['pool'=64,'head'=8] {'pool'}, dimensions={0}, use_global_device_ids=true | all-gather | bytes 33280 | tf_op jit(solution)/shard_map/all_gather | solution.py:17
  289.7 1055.2 %while.35 = (s32[]{:T(128)}, f32[1,192]{1,0:T(1,128)S(1)}, f32[1,192]{1,0:T(1,128)S(1)}, f32[1,192,128]{2,1,0:T(8,128)S(1)}, s32[128]{0:T(128)S(1)}, /*index=5*/...) while((s32[]{:T(128)}, f32[1,192]{1,0:T(1,128)S(1)}, ...), condition=%wide.region_11.12_spmd.clone, body=%wide.region_6.11_spmd.clone.sunk | while | flops 6599373 | bytes 545140 | solution.py:194
  326.5 6.3 conditional.7
  337.9 6.3 conditional.7
  349.3 6.3 conditional.7
  360.7 6.3 conditional.7
  377.2 6.3 conditional.7
  388.6 6.3 conditional.7
  458.4 6.3 conditional.7
  469.8 6.3 conditional.7
  481.2 6.3 conditional.7
  558.5 6.3 conditional.7
  667.6 6.3 conditional.7
  854.1 6.3 conditional.7
  963.1 6.3 conditional.7
  1053.2 6.3 conditional.7
  1087.4 6.3 conditional.7
  1181.2 6.3 conditional.7
  1310.6 6.3 conditional.7
  1338.5 6.3 conditional.7
  1346.5 66.8 %while.34 = (s32[]{:T(128)}, f32[1,256]{1,0:T(1,128)S(1)}, f32[1,256]{1,0:T(1,128)S(1)}, f32[1,256,128]{2,1,0:T(8,128)S(1)}, bf16[64,1,256]{2,1,0:T(2,128)(2,1)S...) while((s32[]{:T(128)}, f32[1,256]{1,0:T(1,128)S(1)}, ...), condition=%wide.region_23.24_spmd, body=%wide.region_22.23_spmd.sunk | while | flops 133125 | bytes 337047 | solution.py:25
  1413.8 24.1 %psum.7 = bf16[32,128]{1,0:T(8,128)(2,1)} all-reduce(f32[32,128]{1,0:T(8,128)S(1)} %fusion.141), channel_id=1, replica_groups=mesh['pool'=64,'head'=8] {'head'}, use_global_device_ids=true, to_apply=%region_26.27 | all-reduce | flops 4096 | bytes 24576 | tf_op jit(solution)/shard_map/psum | solution.py:237
  (1737 shorter events, 867.4 us)
Async XLA Ops:
  7.2 1406.5 %copy-start = (bf16[1024,128]{1,0:T(8,128)(2,1)S(1)}, bf16[1024,128]{1,0:T(8,128)(2,1)}, u32[]{:S(2)}) copy-start(bf16[1024,128]{1,0:T(8,128)(2,1)} %param.26) | copy-start | bytes 786436
  7.2 282.5 %all-gather.8.cloned.1.call-start = ((), (), s32[]{:S(2)}) async-start(), calls=%async_computation | async-start | bytes 4259840 | tf_op jit(solution)/shard_map/all_gather | solution.py:178
  7.9 1337.7 %all-gather.10.cloned.1.call-start = ((), (), s32[]{:S(2)}) async-start(), calls=%async_computation.1 | async-start | bytes 4259840 | tf_op jit(solution)/shard_map/all_gather | solution.py:17
  110.9 4.5 copy-start.1
  114.6 0.9 copy-start.5
  114.8 6.6 copy-start.4
  115.1 7.0 copy-start.2
  288.7 0.7 copy-start.3
Sparse Core Ops, SparseCore 0:
  10.9 141.0 all-gather.7
  154.9 140.6 all-gather.9
where the time goes:
time: 1470 us; the launch traced here: 1440 us
  loops' own time  579 us (39%)
  local copies, waits for them, and re-layouts  303 us (21%)
  blocking collectives  281 us (19%)
  other arithmetic  184 us (13%)
  matrix products  81.1 us (6%)
  between operations  15.7 us (1%)
    another operation x1, loops' own time, shards(): result, _ = lax.scan(one_row, initial, (piece, indices))  406 us
    another operation x128, loops' own time, one_row(): lax.cond(store_live[index] & wanted(place), apply, lambda state_in: state...  169 us
    all_gather x2, blocking collectives, merged_2(): lax.all_gather(part.astype(kind), axis)  164 us
    all_gather x1, blocking collectives, shards(): every_fresh = lax.all_gather(fresh_kv, 'pool', axis=0, tiled=True)  92.9 us
    dynamic_slice x128, local copies, waits for them, and re-layouts, shards(): result, _ = lax.scan(one_row, initial, (piece, indices))  82.3 us
    dynamic_slice x128, local copies, waits for them, and re-layouts, one_row(): place = store_place[index]  81.7 us
    dynamic_slice x128, local copies, waits for them, and re-layouts, one_row(): store_live[index] & wanted(place)  78.2 us
    dot_general x68, matrix products, absorb(): jnp.einsum('gqk,gkd->gqd', weights.astype(jnp.bfloat16), value_block, pre...  66.1 us
  transfers between devices with their start and end apart: 2, of which 0 were waited for; matrix products, arithmetic and copies ran while one was open for 35% of the time, Pallas kernels for 0%

commit v1 on v0

--- a/solution.py
+++ b/solution.py
@@ -141,7 +141,9 @@
     )
     queries = to_groups(rotated_q.reshape(R, -1), group)
     query_reach = jnp.repeat(query_place, group)
-    every_fresh = lax.all_gather(fresh_kv, "pool", axis=0, tiled=True)
+    every_fresh = jnp.concatenate(
+        lax.all_to_all(jnp.stack([fresh_kv] * lax.axis_size("pool")), "pool", 0, 0), axis=0
+    )
     fresh_place = (span_start[:, None] + pick).reshape(-1)
     turned_fresh = rotate(
         every_fresh[:, :, 0].reshape(slots * R, -1, HD).astype(jnp.float32), fresh_place

time: 1470 us -> 1420 us (0.966)
  blocking collectives: 281 us -> 190 us
  waiting for transfers between devices: 0.72 us -> 40 us
    all_gather x1 -> x0, blocking collectives: 92.9 us -> none  [shards(): every_fresh = lax.all_gather(fresh_kv, 'pool', axis=0, tiled=True)]
    all_to_all x0 -> x1, waiting for transfers between devices: none -> 39.3 us  [shards(): lax.all_to_all(jnp.stack([fresh_kv] * lax.axis_size('pool')), 'pool', 0, 0)]
  transfers between devices with their start and end apart: 2 -> 3, of which waited for: 0 -> 1; matrix products, arithmetic and copies ran while one was open for 35% -> 36% of each run, Pallas kernels for 0% -> 0%
where the time goes in v1:
time: 1420 us; the launch traced here: 1400 us
  loops' own time  579 us (41%)
  local copies, waits for them, and re-layouts  301 us (21%)
  blocking collectives  190 us (13%)
  other arithmetic  182 us (13%)
  matrix products  81.1 us (6%)
  waiting for transfers between devices  40 us (3%)
  between operations  15.6 us (1%)
    another operation x1, loops' own time, shards(): result, _ = lax.scan(one_row, initial, (piece, indices))  406 us
    another operation x128, loops' own time, one_row(): lax.cond(store_live[index] & wanted(place), apply, lambda state_in: state...  169 us
    all_gather x2, blocking collectives, merged_2(): lax.all_gather(part.astype(kind), axis)  166 us
    dynamic_slice x128, local copies, waits for them, and re-layouts, shards(): result, _ = lax.scan(one_row, initial, (piece, indices))  82.3 us
    dynamic_slice x128, local copies, waits for them, and re-layouts, one_row(): place = store_place[index]  81.7 us
    dynamic_slice x128, local copies, waits for them, and re-layouts, one_row(): store_live[index] & wanted(place)  78.2 us
    dot_general x68, matrix products, absorb(): jnp.einsum('gqk,gkd->gqd', weights.astype(jnp.bfloat16), value_block, pre...  66.1 us
    add x63, other arithmetic, combine(): first[2] * left[..., None] + second[2] * right[..., None]  63.3 us
  transfers between devices with their start and end apart: 3, of which 1 were waited for; matrix products, arithmetic and copies ran while one was open for 36% of the time, Pallas kernels for 0%

profile of v1, /device:TPU:504, one launch (start us, length us, event | category | flops | bytes accessed | tf_op | source)
XLA Modules:
  0.0 1399.5 jit_solution(17000625714931034058)
XLA Ops:
  9.6 12.1 all-to-all-start
  25.5 39.3 %all-to-all-done = bf16[64,1,24,2,128]{4,2,3,1,0:T(8,128)(2,1)S(1)} async-done(((bf16[64,1,24,2,128]{4,2,3,1,0:T(8,128)(2,1)}), bf16[64,1,24,2,128]{4,2,3,1,0:T(8,128)(2,1)S(1)}, u32[]{:S(2)}, u32[]{:S(2)}) %all-to-all-start) | async-done | bytes 786464 | tf_op jit(solution)/shard_map/all_to_all | solution.py:145
  77.3 87.2 %all-gather.3 = bf16[64,1,256]{2,1,0:T(2,128)(2,1)S(1)} all-gather(bf16[1,1,256]{2,1,0:T(2,128)(2,1)S(1)} %convert_bitcast_fusion.2), channel_id=2, replica_groups=mesh['pool'=64,'head'=8] {'pool'}, dimensions={0}, use_global_device_ids=true | all-gather | bytes 33280 | tf_op jit(solution)/shard_map/all_gather | solution.py:17
  164.5 78.4 %all-gather.4 = bf16[64,1,256]{2,1,0:T(2,128)(2,1)S(1)} all-gather(bf16[1,1,256]{2,1,0:T(2,128)(2,1)S(1)} %convert_bitcast_fusion.1), channel_id=3, replica_groups=mesh['pool'=64,'head'=8] {'pool'}, dimensions={0}, use_global_device_ids=true | all-gather | bytes 33280 | tf_op jit(solution)/shard_map/all_gather | solution.py:17
  244.4 1055.3 %while.35 = (s32[]{:T(128)}, f32[1,192]{1,0:T(1,128)S(1)}, f32[1,192]{1,0:T(1,128)S(1)}, f32[1,192,128]{2,1,0:T(8,128)S(1)}, s32[128]{0:T(128)S(1)}, /*index=5*/...) while((s32[]{:T(128)}, f32[1,192]{1,0:T(1,128)S(1)}, ...), condition=%wide.region_11.12_spmd.clone, body=%wide.region_6.11_spmd.clone.sunk | while | flops 6599373 | bytes 545140 | solution.py:196
  254.5 6.3 conditional.7
  380.1 6.3 conditional.7
  401.6 6.3 conditional.7
  462.5 6.3 conditional.7
  546.2 6.3 conditional.7
  567.8 6.3 conditional.7
  622.3 6.3 conditional.7
  666.7 6.3 conditional.7
  726.3 6.3 conditional.7
  742.8 6.3 conditional.7
  786.0 6.3 conditional.7
  841.7 6.3 conditional.7
  879.8 6.3 conditional.7
  906.4 6.3 conditional.7
  1162.6 6.3 conditional.7
  1194.3 6.3 conditional.7
  1242.5 6.3 conditional.7
  1301.2 66.8 %while.34 = (s32[]{:T(128)}, f32[1,256]{1,0:T(1,128)S(1)}, f32[1,256]{1,0:T(1,128)S(1)}, f32[1,256,128]{2,1,0:T(8,128)S(1)}, bf16[64,1,256]{2,1,0:T(2,128)(2,1)S...) while((s32[]{:T(128)}, f32[1,256]{1,0:T(1,128)S(1)}, ...), condition=%wide.region_23.24_spmd, body=%wide.region_22.23_spmd.sunk | while | flops 133125 | bytes 337047 | solution.py:25
  1368.6 24.1 %psum.7 = bf16[32,128]{1,0:T(8,128)(2,1)} all-reduce(f32[32,128]{1,0:T(8,128)S(1)} %fusion.141), channel_id=1, replica_groups=mesh['pool'=64,'head'=8] {'head'}, use_global_device_ids=true, to_apply=%region_26.27 | all-reduce | flops 4096 | bytes 24576 | tf_op jit(solution)/shard_map/psum | solution.py:239
  (1748 shorter events, 868.6 us)
Async XLA Ops:
  7.2 1361.2 %copy-start = (bf16[1024,128]{1,0:T(8,128)(2,1)S(1)}, bf16[1024,128]{1,0:T(8,128)(2,1)}, u32[]{:S(2)}) copy-start(bf16[1024,128]{1,0:T(8,128)(2,1)} %param.26) | copy-start | bytes 786436
  7.2 237.2 %all-gather.8.cloned.1.call-start = ((), (), s32[]{:S(2)}) async-start(), calls=%async_computation.1 | async-start | bytes 4259840 | tf_op jit(solution)/shard_map/all_gather | solution.py:180
  8.6 13.2 copy-start.1
  8.6 13.3 copy-start.3
  8.6 13.4 copy-start.7
  9.6 12.6 copy-start.9
  9.6 14.5 %copy-start.6 = (s32[32]{0:T(128)S(1)}, s32[32]{0:T(128)}, u32[]{:S(2)}) copy-start(s32[32]{0:T(128)} %param.31) | copy-start | bytes 388
  9.6 14.7 %copy-start.8 = (s32[64]{0:T(128)S(1)}, s32[64]{0:T(128)}, u32[]{:S(2)}) copy-start(s32[64]{0:T(128)} %param.28) | copy-start | bytes 772
  9.6 15.9 %copy-start.2 = (bf16[2,2,64,128]{3,2,1,0:T(8,128)(2,1)S(1)}, bf16[2,2,64,128]{3,2,1,0:T(8,128)(2,1)}, u32[]{:S(2)}) copy-start(bf16[2,2,64,128]{3,2,1,0:T(8,128)(2,1)} %param.21) | copy-start | bytes 196612
  9.6 55.2 %all-to-all-start = ((bf16[64,1,24,2,128]{4,2,3,1,0:T(8,128)(2,1)}), bf16[64,1,24,2,128]{4,2,3,1,0:T(8,128)(2,1)S(1)}, u32[]{:S(2)}, u32[]{:S(2)}) async-start(bf16[64,1,24,2,128]{4,2,3,1,0:T(8,128)(2,1)} %stack.2), calls=%async_computation | async-start | bytes 1572864 | tf_op jit(solution)/shard_map/all_to_all | solution.py:145
  21.8 1278.6 %all-gather.10.cloned.1.call-start = ((), (), s32[]{:S(2)}) async-start(), calls=%async_computation.2 | async-start | bytes 4259840 | tf_op jit(solution)/shard_map/all_gather | solution.py:17
  68.9 6.1 copy-start.5
  69.2 7.9 copy-start.4
Sparse Core Ops, SparseCore 0:
  10.9 146.2 all-gather.7
  160.1 140.9 all-gather.9
